TPU v7x, 32 devices: a whole 2x2x4 slice. The times are simulated.
32 devices in a mesh: group: 2 (over x), wide: 8 (over z, y), narrow: 2 (over core).
Axes of the slice: x: 2, y: 2, z: 4, core: 2. Of those that a mesh axis runs over, the one named last changes fastest.
Arguments:
- voxels: bfloat16 [65536, 512], P(('group', 'wide', 'narrow')), parts along dimension 0, may hold values from -6 to 6
- w_qkv: bfloat16 [512, 1536], replicated, may hold values from -0.25 to 0.25
- w_out: bfloat16 [512, 512], replicated, may hold values from -0.25 to 0.25
- w_feature: bfloat16 [512, 256], replicated, may hold values from -0.25 to 0.25
- conv_first: bfloat16 [3, 3, 256, 256], replicated, may hold values from -0.125 to 0.125
- conv_second: bfloat16 [3, 3, 256, 256], replicated, may hold values from -0.125 to 0.125
- row_brick: int32 [512, 1], P(('group', 'wide', 'narrow')), parts along dimension 0, may hold values from 0 to 7; in each aligned block of 16 rows (0 to 15, 16 to 31, ...) at most 4 rows name the same one
- cell_place: int32 [65536], P(('group', 'wide', 'narrow')), parts along dimension 0, may hold values from 0 to 255
Outputs:
- flow_field: float32 [128, 64, 256], P(('group', 'wide'), 'narrow'), parts along dimension 0
There are 2 independent parts, one for each index of `group`. A program takes and returns all parts, laid end to end along the dimension named above; an argument that names none is the same for every part. Nothing has to cross between parts.
Inputs may be any that keep to these rules, and one draw needn't show every extreme that they name: `row_brick`: within the rows of one device (16 rows in a row), no brick row is named more than 4 times, and some brick row exactly 4 times.
All inputs are finite; a program needn't handle non-finite values.
Results may differ from a plain program's by a relative error of at most 0.014.
Values may be sent and summed in bfloat16 or wider, within the bound.
A program may use at most 128 MiB of HBM per device.

v0:
```python
import functools
import math

import jax
import jax.numpy as jnp
from jax import lax
from jax.experimental import pallas as pl
from jax.experimental.pallas import tpu as pltpu
from jax.sharding import PartitionSpec as P

D = 512
HEADS = 4
HEAD = 128
PF = 256
ROW = 128
BLK = 256
BX = 8
BY = 32
CELLS = BX * BY
PAIR = 2 * HEAD
EDGE = 16
WIDTH = BY + 2 * EDGE
HALO = 2
PIECES = 4
PIECE = CELLS // PIECES

epsilon = 1e-06
MESH = pl.DeviceIdType.MESH
F32 = jnp.float32
BF16 = jnp.bfloat16


def dot(a, b):
    return jnp.dot(a, b, preferred_element_type=F32)


def dot_t(a, b):
    return lax.dot_general(a, b, (((0,), (0,)), ((), ())), preferred_element_type=F32)


def dot_nt(a, b):
    return lax.dot_general(a, b, (((1,), (1,)), ((), ())), preferred_element_type=F32)


def kernel(
    wide_count, narrow_count, token_count,
    vox_hbm, wqkv_hbm, wout_hbm, wfeat_hbm, first_hbm, second_hbm, brick_ref, cell_ref,
    out_ref,
    vox, wqkv, wout, wfeat, first, second,
    kv, qs, att, within, total, feats, keys,
    own_total, quad_parts, quad_send, quad_recv, prefix_send, prefix_recv,
    part_send, part_recv, own_part,
    pooled, ext, rows_recv, cols_recv, corner_recv, inner,
    vox_sem, load_sem,
    s1, r1, s2, r2, s3, r3, sa, ra, sh, rh,
):
    blocks = token_count // BLK
    quads = wide_count // 2
    bits = wide_count.bit_length() - 1
    wide = lax.axis_index("wide")
    narrow = lax.axis_index("narrow")
    side = wide % 2
    quad = wide // 2
    members = 2 * narrow_count
    place = side * narrow_count + narrow

    def load_vox(b):
        span = pl.ds(pl.multiple_of(b * BLK, BLK), BLK)
        return pltpu.make_async_copy(vox_hbm.at[span], vox.at[span], vox_sem.at[b])

    def load(source, target, k):
        return pltpu.make_async_copy(source, target, load_sem.at[k])

    loads = [
        load(wqkv_hbm.at[:, pl.ds(D, 2 * D)], wqkv.at[:, pl.ds(D, 2 * D)], 0),
        load(wout_hbm, wout, 1),
        load(wfeat_hbm, wfeat, 2),
        load(first_hbm, first, 3),
        load(second_hbm, second, 4),
        load(wqkv_hbm.at[:, pl.ds(0, D)], wqkv.at[:, pl.ds(0, D)], 5),
    ]
    loads[0].start()
    for b in range(blocks):
        load_vox(b).start()
    for k in (5, 1, 2, 3, 4):
        loads[k].start()

    everyone = wide_count * narrow_count
    me = wide * narrow_count + narrow
    barrier = pltpu.get_barrier_semaphore()

    def greet(k, carry):
        other = (me + k) % everyone
        pl.semaphore_signal(
            barrier, inc=1,
            device_id={"wide": other // narrow_count, "narrow": other % narrow_count},
            device_id_type=MESH,
        )
        return carry

    lax.fori_loop(1, everyone, greet, 0)

    def remote(source, target, send_sem, recv_sem, to_wide, to_narrow):
        return pltpu.make_async_remote_copy(
            src_ref=source, dst_ref=target, send_sem=send_sem, recv_sem=recv_sem,
            device_id={"wide": to_wide, "narrow": to_narrow}, device_id_type=MESH,
        )

    same_head = (
        lax.broadcasted_iota(jnp.int32, (PAIR, PAIR), 0) // HEAD
        == lax.broadcasted_iota(jnp.int32, (PAIR, PAIR), 1) // HEAD
    )
    causal = lax.broadcasted_iota(jnp.int32, (BLK, BLK), 0) >= lax.broadcasted_iota(
        jnp.int32, (BLK, BLK), 1
    )
    rows = token_count // ROW
    level = lax.broadcasted_iota(jnp.int32, (rows, rows), 0) == lax.broadcasted_iota(
        jnp.int32, (rows, rows), 1
    )
    bricks = jnp.sum(
        jnp.where(level, jnp.broadcast_to(brick_ref[...].astype(F32), (rows, rows)), 0.0),
        axis=1, keepdims=True,
    ).astype(jnp.int32)
    keys[...] = cell_ref[...] + bricks * CELLS
    ext[...] = jnp.zeros_like(ext)
    total[...] = jnp.zeros_like(total)
    loads[0].wait()

    def keys_values(b, carry):
        load_vox(b).wait()
        span = pl.ds(pl.multiple_of(b * BLK, BLK), BLK)
        both = dot(vox[span, :], wqkv[:, D:]).astype(BF16)
        kv[span, :] = both
        for p in range(HEADS // 2):
            columns = slice(p * PAIR, (p + 1) * PAIR)
            before = total[p]
            within[b, p] = before.astype(BF16)
            state = dot_t(both[:, columns], both[:, D:][:, columns])
            total[p] = before + jnp.where(same_head, state, 0.0)
        return carry

    lax.fori_loop(0, blocks, keys_values, 0, unroll=4)

    for h in range(HEADS):
        corner = slice((h % 2) * HEAD, (h % 2 + 1) * HEAD)
        own_total[h] = total[h // 2, corner, corner].astype(BF16)
    pl.semaphore_wait(barrier, everyone - 1)

    def member(t):
        other = (place + t) % members
        return other, quad * 2 + other // narrow_count, other % narrow_count

    def gather_copy(t):
        other, to_wide, to_narrow = member(t)
        return remote(
            own_total.at[other], quad_parts.at[t - 1], s1.at[t - 1], r1.at[t - 1], to_wide, to_narrow
        )

    for t in range(1, members):
        gather_copy(t).start()

    def local(b, carry):
        span = pl.ds(pl.multiple_of(b * BLK, BLK), BLK)
        query = dot(vox[span, :], wqkv[:, :D]).astype(BF16)
        qs[span, :] = query
        for p in range(HEADS // 2):
            columns = slice(p * PAIR, (p + 1) * PAIR)
            carried = dot(query[:, columns], within[b, p])
            for i in range(2):
                h = 2 * p + i
                mine = slice(h * HEAD, (h + 1) * HEAD)
                scores = dot_nt(query[:, mine], kv[span, mine])
                scores = jnp.where(causal, scores, 0.0).astype(BF16)
                att[span, mine] = carried[:, i * HEAD:(i + 1) * HEAD] + dot(
                    scores, kv[span, D + h * HEAD:D + (h + 1) * HEAD]
                )
        return carry

    cut_one = blocks // 4
    cut_two = (3 * blocks) // 4
    loads[5].wait()
    lax.fori_loop(0, cut_one, local, 0, unroll=2)

    for t in range(1, members):
        gather_copy(t).wait_recv()
    mine_total = own_total[place].astype(F32)
    quad_sum = mine_total
    for t in range(1, members):
        quad_sum = quad_sum + quad_parts[t - 1].astype(F32)
    quad_send[...] = quad_sum.astype(BF16)

    def later_copy(t):
        return remote(
            quad_send, quad_recv.at[t - 1], s2.at[t - 1], r2.at[t - 1],
            ((quad + t) % quads) * 2 + side, narrow,
        )

    for t in range(1, quads):
        @pl.when(quad + t < quads)
        def _(t=t):
            later_copy(t).start()

    lax.fori_loop(cut_one, cut_two, local, 0, unroll=4)

    prefix_own = jnp.zeros((HEAD, HEAD), F32)
    total[0, :HEAD, :HEAD] = prefix_own
    for t in range(1, quads):
        @pl.when(quad - t >= 0)
        def _(t=t):
            later_copy(t).wait_recv()
            total[0, :HEAD, :HEAD] = total[0, :HEAD, :HEAD] + quad_recv[t - 1].astype(F32)
    base = total[0, :HEAD, :HEAD]

    def part_of(m):
        value = mine_total
        for t in range(1, members):
            value = jnp.where((place - t + members) % members == m, quad_parts[t - 1].astype(F32), value)
        return value

    running = base
    for m in range(members):
        prefix_send[m] = running.astype(BF16)
        if m < members - 1:
            running = running + part_of(m)

    def spread_copy(t):
        other, to_wide, to_narrow = member(t)
        return remote(
            prefix_send.at[other], prefix_recv.at[place], s3.at[t - 1], r3.at[t - 1], to_wide, to_narrow
        )

    def spread_arrival(t):
        source = (place - t + members) % members
        return remote(
            prefix_send.at[source], prefix_recv.at[source], s3.at[t - 1], r3.at[t - 1], wide, narrow
        )

    for t in range(1, members):
        spread_copy(t).start()
    prefix_recv[place] = prefix_send[place]

    lax.fori_loop(cut_two, blocks, local, 0, unroll=2)

    for t in range(1, members):
        spread_arrival(t).wait_recv()
    blank = jnp.zeros((HEAD, HEAD), BF16)
    prefixes = []
    for p in range(HEADS // 2):
        upper = jnp.concatenate([prefix_recv[2 * p], blank], axis=1)
        lower = jnp.concatenate([blank, prefix_recv[2 * p + 1]], axis=1)
        within[0, p] = jnp.concatenate([upper, lower], axis=0)

    loads[1].wait()
    loads[2].wait()

    def project(b, carry):
        span = pl.ds(pl.multiple_of(b * BLK, BLK), BLK)
        pieces = []
        for p in range(HEADS // 2):
            columns = slice(p * PAIR, (p + 1) * PAIR)
            attended = att[span, columns] + dot(qs[span, columns], within[0, p])
            for i in range(2):
                one = attended[:, i * HEAD:(i + 1) * HEAD]
                square = jnp.mean(one * one, axis=-1, keepdims=True)
                pieces.append((one * lax.rsqrt(square + epsilon)).astype(BF16))
        normed = jnp.concatenate(pieces, axis=1)
        hidden = (vox[span, :].astype(F32) + dot(normed, wout[...])).astype(BF16)
        feats[span, :] = dot(hidden, wfeat[...]).astype(BF16)
        return carry

    lax.fori_loop(0, blocks, project, 0, unroll=4)

    cell_ids = lax.broadcasted_iota(jnp.int32, (CELLS, ROW), 0)

    def partial_pool(brick):
        wanted = cell_ids + brick * CELLS
        marks = [
            jnp.where(keys[r:r + 1, :] == wanted, 1.0, 0.0).astype(BF16)
            for r in range(token_count // ROW)
        ]
        return dot(jnp.concatenate(marks, axis=1), feats[...])

    def across(r):
        target = wide
        for s in range(bits):
            target = target + (r // 2**s) % 2 * 2**s * (1 - 2 * ((wide // 2**s) % 2))
        return target

    def piece_copy(r, bit, k):
        rows = pl.ds(k * PIECE, PIECE)
        return remote(
            part_send.at[r - 1, rows], part_recv.at[r - 1, rows],
            sa.at[r - 1, k], ra.at[r - 1, k], across(bit), narrow,
        )

    def pool_for_partner(i, carry):
        r = wide_count - 1 - 2 * i
        part_send[r - 1] = partial_pool(across(r)).astype(BF16)
        for k in range(PIECES):
            piece_copy(r, 1, k).start()
        return carry

    lax.fori_loop(0, wide_count // 2, pool_for_partner, 0)

    def pool_own(i, carry):
        own_part[wide_count // 2 - 1 - i] = partial_pool(across(wide_count - 2 - 2 * i))
        return carry

    lax.fori_loop(0, wide_count // 2, pool_own, 0)

    for r in range(wide_count - 2, -1, -2):
        low = r & -r if r else wide_count
        for k in range(PIECES):
            span = slice(k * PIECE, (k + 1) * PIECE)
            summed = own_part[r // 2, span]
            bit = 1
            while bit < low:
                piece_copy(r + bit, bit, k).wait_recv()
                summed = summed + part_recv[r + bit - 1, span].astype(F32)
                bit *= 2
            if r:
                part_send[r - 1, span] = summed.astype(BF16)
                piece_copy(r, low, k).start()
            else:
                own_part[0, span] = summed
    grid_sum = own_part[0]
    pooled[...] = grid_sum.astype(BF16).reshape(BX, BY, PF)

    def halo_copy(k, dy, dx):
        if dy == 0:
            source = pooled.at[:, pl.ds(BY - EDGE if dx > 0 else 0, EDGE)]
            target = cols_recv.at[0 if dx > 0 else 1]
        else:
            rows = pl.ds(BX - HALO if dy > 0 else 0, HALO)
            if dx == 0:
                source = pooled.at[rows]
                target = rows_recv.at[0 if dy > 0 else 1]
            else:
                source = pooled.at[rows, pl.ds(BY - EDGE if dx > 0 else 0, EDGE)]
                target = corner_recv.at[(0 if dy > 0 else 2) + (0 if dx > 0 else 1)]
        return remote(
            source, target, sh.at[k], rh.at[k],
            (wide + dy + wide_count) % wide_count, (narrow + dx + narrow_count) % narrow_count,
        )

    steps = [(dy, dx) for dy in (-1, 1) for dx in (0, -1, 1)] + [(0, -1), (0, 1)]

    def inside(dy, dx):
        return (
            (wide + dy >= 0) & (wide + dy < wide_count)
            & (narrow + dx >= 0) & (narrow + dx < narrow_count)
        )

    for k, (dy, dx) in enumerate(steps):
        @pl.when(inside(dy, dx))
        def _(k=k, dy=dy, dx=dx):
            halo_copy(k, dy, dx).start()

    ext[HALO:HALO + BX, EDGE:EDGE + BY, :] = pooled[...]
    loads[3].wait()
    loads[4].wait()
    for k, (dy, dx) in enumerate(steps):
        @pl.when(inside(-dy, -dx))
        def _(k=k, dy=dy, dx=dx):
            halo_copy(k, dy, dx).wait_recv()
            rows = slice(HALO, HALO + BX)
            if dy > 0:
                rows = slice(0, HALO)
            elif dy < 0:
                rows = slice(HALO + BX, 2 * HALO + BX)
            if dx == 0:
                ext[rows, EDGE:EDGE + BY, :] = rows_recv[0 if dy > 0 else 1]
            else:
                columns = slice(0, EDGE) if dx > 0 else slice(EDGE + BY, WIDTH)
                if dy == 0:
                    ext[rows, columns, :] = cols_recv[0 if dx > 0 else 1]
                else:
                    ext[rows, columns, :] = corner_recv[(0 if dy > 0 else 2) + (0 if dx > 0 else 1)]

    def convolve(field, weight, height):
        size = height * WIDTH
        result = None
        for dx in range(3):
            shifted = None
            for dy in range(3):
                window = field[dy:dy + height].reshape(size, PF)
                term = dot(window, weight[dy, dx])
                shifted = term if shifted is None else shifted + term
            if dx != 1:
                shifted = pltpu.roll(shifted, 1 if dx == 0 else size - 1, 0)
            result = shifted if result is None else result + shifted
        return result.reshape(height, WIDTH, PF)

    tall = BX + 2
    active = jax.nn.gelu(convolve(ext, first, tall), approximate=True)
    grid_row = lax.broadcasted_iota(jnp.int32, (tall, WIDTH, PF), 0) + wide * BX - 1
    grid_column = lax.broadcasted_iota(jnp.int32, (tall, WIDTH, PF), 1) + narrow * BY - EDGE
    real = (
        (grid_row >= 0) & (grid_row < wide_count * BX)
        & (grid_column >= 0) & (grid_column < narrow_count * BY)
    )
    inner[...] = jnp.where(real, active, 0.0).astype(BF16)
    out_ref[...] = convolve(inner, second, BX)[:, EDGE:EDGE + BY, :]

    for t in range(1, members):
        gather_copy(t).wait_send()
        spread_copy(t).wait_send()
    for t in range(1, quads):
        @pl.when(quad + t < quads)
        def _(t=t):
            later_copy(t).wait_send()

    for r in range(1, wide_count):
        for k in range(PIECES):
            piece_copy(r, r & -r, k).wait_send()
    for k, (dy, dx) in enumerate(steps):
        @pl.when(inside(dy, dx))
        def _(k=k, dy=dy, dx=dx):
            halo_copy(k, dy, dx).wait_send()


def per_device(voxels, w_qkv, w_out, w_feature, conv_first, conv_second, row_brick, cell_place):
    token_count = voxels.shape[0]
    rows = token_count // ROW
    wide_count = lax.axis_size("wide")
    narrow_count = lax.axis_size("narrow")
    blocks = token_count // BLK
    quads = wide_count // 2
    members = 2 * narrow_count
    others = max(1, quads - 1)
    anywhere = pl.BlockSpec(memory_space=pl.ANY)
    vmem = pl.BlockSpec(memory_space=pltpu.VMEM)
    dma = pltpu.SemaphoreType.DMA
    state = (HEAD, HEAD)
    grid = (CELLS, PF)
    scratch = [
        pltpu.VMEM(voxels.shape, BF16),
        pltpu.VMEM(w_qkv.shape, BF16),
        pltpu.VMEM(w_out.shape, BF16),
        pltpu.VMEM(w_feature.shape, BF16),
        pltpu.VMEM(conv_first.shape, BF16),
        pltpu.VMEM(conv_second.shape, BF16),
        pltpu.VMEM((token_count, 2 * D), BF16),
        pltpu.VMEM((token_count, D), BF16),
        pltpu.VMEM((token_count, D), F32),
        pltpu.VMEM((blocks, HEADS // 2, PAIR, PAIR), BF16),
        pltpu.VMEM((HEADS // 2, PAIR, PAIR), F32),
        pltpu.VMEM((token_count, PF), BF16),
        pltpu.VMEM((rows, ROW), jnp.int32),
        pltpu.VMEM((members,) + state, BF16),
        pltpu.VMEM((members,) + state, BF16),
        pltpu.VMEM(state, BF16),
        pltpu.VMEM((others,) + state, BF16),
        pltpu.VMEM((members,) + state, BF16),
        pltpu.VMEM((members,) + state, BF16),
        pltpu.VMEM((wide_count - 1,) + grid, BF16),
        pltpu.VMEM((wide_count - 1,) + grid, BF16),
        pltpu.VMEM((quads,) + grid, F32),
        pltpu.VMEM((BX, BY, PF), BF16),
        pltpu.VMEM((BX + 2 * HALO, WIDTH, PF), BF16),
        pltpu.VMEM((2, HALO, BY, PF), BF16),
        pltpu.VMEM((2, BX, EDGE, PF), BF16),
        pltpu.VMEM((4, HALO, EDGE, PF), BF16),
        pltpu.VMEM((BX + 2, WIDTH, PF), BF16),
        dma((blocks,)),
        dma((6,)),
        dma((members - 1,)), dma((members - 1,)),
        dma((others,)), dma((others,)),
        dma((members - 1,)), dma((members - 1,)),
        dma((wide_count - 1, PIECES)), dma((wide_count - 1, PIECES)),
        dma((8,)), dma((8,)),
    ]
    return pl.pallas_call(
        functools.partial(kernel, wide_count, narrow_count, token_count),
        out_shape=jax.ShapeDtypeStruct((BX, BY, PF), F32),
        in_specs=[anywhere] * 6 + [vmem, vmem],
        out_specs=vmem,
        scratch_shapes=scratch,
        compiler_params=pltpu.CompilerParams(
            collective_id=0, has_side_effects=True, vmem_limit_bytes=56 * 1024 * 1024
        ),
        name="scene_flow",
    )(
        voxels, w_qkv, w_out, w_feature, conv_first, conv_second,
        row_brick.reshape(1, rows), cell_place.reshape(rows, ROW),
    )


def solution(mesh):
    placed = (
        P(("group", "wide", "narrow"), None),
        P(),
        P(),
        P(),
        P(),
        P(),
        P(("group", "wide", "narrow"), None),
        P(("group", "wide", "narrow")),
    )
    return jax.shard_map(
        per_device,
        mesh=mesh,
        in_specs=placed,
        out_specs=P(("group", "wide"), "narrow", None),
        check_vma=False,
    )
```

profile of v0, /device:TPU:1, one launch (start us, length us, event | category | flops | bytes accessed | tf_op | source)
XLA Modules:
  0.0 46.9 jit_solution(4049431489709059856)
XLA Ops:
  0.0 45.2 %scene_flow.1 = f32[8,32,256]{2,1,0:T(8,128)} custom-call(bf16[2048,512]{1,0:T(8,128)(2,1)} %vox_hbm.1, bf16[512,1536]{1,0:T(8,128)(2,1)} %wqkv_hbm.1, bf16[512,512]{1,0:T(8,128)(2,1)} %wout_hbm.1, bf16[512,256]{1,0:T(8,128)(2,1)} %wfeat_hbm.1, bf16[3,3,256,256]{3,2,1,0:T(8,128)(2,1)} %first_hbm.1, bf16[3,3,256,256]{3,2,1,0:T(8,128)(2,1)} %second_hbm.1, ...), custom_call_target="tpu_custom_call" | custom-call | tf_op jit(solution)/shard_map/scene_flow/pallas_call | solution.py:473
  45.2 1.7 %copy.10 = f32[8,32,256]{2,1,0:T(8,128)} copy(f32[8,32,256]{2,1,0:T(8,128)} %scene_flow.1) | data formatting | bytes 524288
where the time goes:
time: 47.5 us; the launch traced here: 46.9 us
  Pallas kernels  45.2 us (95%)
  local copies, waits for them, and re-layouts  1.67 us (4%)
    pallas_call x1, Pallas kernels, per_device(): pl.pallas_call(functools.partial(kernel, wide_count, narrow_count, token_...  45.2 us
    unnamed x1, local copies, waits for them, and re-layouts  1.67 us

commit v1 on v0

v1 whole, which is shorter than its diff:
```python
import functools
import math

import jax
import jax.numpy as jnp
from jax import lax
from jax.experimental import pallas as pl
from jax.experimental.pallas import tpu as pltpu
from jax.sharding import PartitionSpec as P

D = 512
HEADS = 4
HEAD = 128
PF = 256
ROW = 128
BLK = 256
BX = 8
BY = 32
CELLS = BX * BY
PAIR = 2 * HEAD
EDGE = 16
WIDTH = BY + 2 * EDGE
HALO = 2
PIECES = 4
PIECE = CELLS // PIECES
PIECE_ORDER = (0, 3, 1, 2)
SWAPPED = 2
PARTS = 2
PART = HEAD // PARTS

epsilon = 1e-06
MESH = pl.DeviceIdType.MESH
F32 = jnp.float32
BF16 = jnp.bfloat16


def dot(a, b):
    return jnp.dot(a, b, preferred_element_type=F32)


def dot_t(a, b):
    return lax.dot_general(a, b, (((0,), (0,)), ((), ())), preferred_element_type=F32)


def dot_nt(a, b):
    return lax.dot_general(a, b, (((1,), (1,)), ((), ())), preferred_element_type=F32)


def diagonal(upper, lower):
    blank_right = jnp.zeros((upper.shape[0], lower.shape[1]), upper.dtype)
    blank_left = jnp.zeros((lower.shape[0], upper.shape[1]), lower.dtype)
    return jnp.concatenate(
        [
            jnp.concatenate([upper, blank_right], axis=1),
            jnp.concatenate([blank_left, lower], axis=1),
        ],
        axis=0,
    )


def swap_bits(label):
    return label - label % 4 + 2 * (label % 2) + (label // 2) % 2


def kernel(
    wide_count, narrow_count, token_count, most,
    vox_hbm, wqkv_hbm, wout_hbm, wfeat_hbm, first_hbm, second_hbm, brick_ref, cell_ref,
    out_ref,
    vox, wqkv, wout, wfeat, first, second,
    kv, qs, att, direct, mixed, within, total, feats, slots,
    own_total, quad_parts, quad_send, quad_recv, prefix_send, prefix_recv,
    part_send, part_recv, own_part,
    pooled, ext, rows_recv, cols_recv, corner_recv, inner,
    vox_sem, load_sem,
    s1, r1, s2, r2, s3, r3, sa, ra, sh, rh,
):
    blocks = token_count // BLK
    rows = token_count // ROW
    quads = wide_count // 2
    bits = wide_count.bit_length() - 1
    wide = lax.axis_index("wide")
    narrow = lax.axis_index("narrow")
    side = wide % 2
    quad = wide // 2
    members = 2 * narrow_count
    place = side * narrow_count + narrow

    def load_vox(b):
        span = pl.ds(pl.multiple_of(b * BLK, BLK), BLK)
        return pltpu.make_async_copy(vox_hbm.at[span], vox.at[span], vox_sem.at[b])

    def load(source, target, k):
        return pltpu.make_async_copy(source, target, load_sem.at[k])

    loads = [
        load(wqkv_hbm.at[:, pl.ds(D, 2 * D)], wqkv.at[:, pl.ds(D, 2 * D)], 0),
        load(wout_hbm, wout, 1),
        load(wfeat_hbm, wfeat, 2),
        load(first_hbm, first, 3),
        load(second_hbm, second, 4),
        load(wqkv_hbm.at[:, pl.ds(0, D)], wqkv.at[:, pl.ds(0, D)], 5),
    ]
    loads[0].start()
    for b in range(blocks):
        load_vox(b).start()
    for k in (5, 2, 1, 3, 4):
        loads[k].start()

    everyone = wide_count * narrow_count
    me = wide * narrow_count + narrow
    barrier = pltpu.get_barrier_semaphore()

    def greet(k, carry):
        other = (me + k) % everyone
        pl.semaphore_signal(
            barrier, inc=1,
            device_id={"wide": other // narrow_count, "narrow": other % narrow_count},
            device_id_type=MESH,
        )
        return carry

    lax.fori_loop(1, everyone, greet, 0)

    def remote(source, target, send_sem, recv_sem, to_wide, to_narrow):
        return pltpu.make_async_remote_copy(
            src_ref=source, dst_ref=target, send_sem=send_sem, recv_sem=recv_sem,
            device_id={"wide": to_wide, "narrow": to_narrow}, device_id_type=MESH,
        )

    causal = lax.broadcasted_iota(jnp.int32, (ROW, PAIR), 0) >= (
        lax.broadcasted_iota(jnp.int32, (ROW, PAIR), 1) % ROW
    )
    total[...] = jnp.zeros_like(total)
    ext[...] = jnp.zeros_like(ext)
    loads[0].wait()

    def keys_values(b, carry):
        load_vox(b).wait()
        span = pl.ds(pl.multiple_of(b * BLK, BLK), BLK)
        both = dot(vox[span, :], wqkv[:, D:]).astype(BF16)
        kv[span, :] = both
        for h in range(HEADS):
            key = both[:, h * HEAD:(h + 1) * HEAD]
            value = both[:, D + h * HEAD:D + (h + 1) * HEAD]
            state = dot_t(key, diagonal(value[:ROW], value[ROW:]))
            before = total[h]
            within[2 * b, h] = before.astype(BF16)
            middle = before + state[:, :HEAD]
            within[2 * b + 1, h] = middle.astype(BF16)
            total[h] = middle + state[:, HEAD:]
        return carry

    lax.fori_loop(0, blocks, keys_values, 0, unroll=4)

    for h in range(HEADS):
        own_total[h] = total[h].astype(BF16)
    pl.semaphore_wait(barrier, everyone - 1)

    def part_rows(j):
        return pl.ds(j * PART, PART)

    def member(t):
        other = (place + t) % members
        return other, quad * 2 + other // narrow_count, other % narrow_count

    def gather_copy(t, j):
        other, to_wide, to_narrow = member(t)
        return remote(
            own_total.at[other, part_rows(j)], quad_parts.at[t - 1, part_rows(j)],
            s1.at[t - 1, j], r1.at[t - 1, j], to_wide, to_narrow,
        )

    for j in range(PARTS):
        for t in range(1, members):
            gather_copy(t, j).start()

    def local(b, carry):
        span = pl.ds(pl.multiple_of(b * BLK, BLK), BLK)
        query = dot(vox[span, :], wqkv[:, :D]).astype(BF16)
        qs[span, :] = query
        direct[span, :] = dot(vox[span, :], wfeat[...])
        for c in range(BLK // ROW):
            chunk = pl.ds(pl.multiple_of(b * BLK + c * ROW, ROW), ROW)
            for p in range(HEADS // 2):
                columns = slice(p * PAIR, (p + 1) * PAIR)
                low, high = 2 * p * HEAD, (2 * p + 1) * HEAD
                keys = diagonal(kv[chunk, low:low + HEAD], kv[chunk, high:high + HEAD])
                scores = dot_nt(query[c * ROW:(c + 1) * ROW, columns], keys)
                scores = jnp.where(causal, scores, 0.0).astype(BF16)
                values = diagonal(
                    kv[chunk, D + low:D + low + HEAD], kv[chunk, D + high:D + high + HEAD]
                )
                att[chunk, columns] = dot(scores, values)
        return carry

    cut = blocks // 2
    loads[5].wait()
    loads[2].wait()
    lax.fori_loop(0, cut, local, 0, unroll=2)

    def later_copy(t, j):
        return remote(
            quad_send.at[part_rows(j)], quad_recv.at[t - 1, part_rows(j)],
            s2.at[t - 1, j], r2.at[t - 1, j],
            ((quad + t) % quads) * 2 + side, narrow,
        )

    for j in range(PARTS):
        piece = slice(j * PART, (j + 1) * PART)
        for t in range(1, members):
            gather_copy(t, j).wait_recv()
        quad_sum = own_total[place, piece].astype(F32)
        for t in range(1, members):
            quad_sum = quad_sum + quad_parts[t - 1, piece].astype(F32)
        quad_send[piece] = quad_sum.astype(BF16)
        for t in range(1, quads):
            @pl.when(quad + t < quads)
            def _(t=t, j=j):
                later_copy(t, j).start()

    lax.fori_loop(cut, blocks, local, 0, unroll=2)
    loads[1].wait()
    mixed[...] = dot(wout[...], wfeat[...]).astype(BF16)

    def assign(b, carry):
        held = [jnp.int32(-1)] * most
        for r in range(rows):
            hit = brick_ref[0, r] == b
            held = [
                jnp.where(hit, jnp.int32(r) if m == 0 else held[m - 1], held[m]) for m in range(most)
            ]
        for m in range(most):
            slots[b * most + m] = held[m]
        return carry

    lax.fori_loop(0, wide_count, assign, 0)

    def spread_copy(t, j):
        other, to_wide, to_narrow = member(t)
        return remote(
            prefix_send.at[other, part_rows(j)], prefix_recv.at[place, part_rows(j)],
            s3.at[t - 1, j], r3.at[t - 1, j], to_wide, to_narrow,
        )

    def spread_arrival(t, j):
        source = (place - t + members) % members
        return remote(
            prefix_send.at[source, part_rows(j)], prefix_recv.at[source, part_rows(j)],
            s3.at[t - 1, j], r3.at[t - 1, j], wide, narrow,
        )

    for j in range(PARTS):
        piece = slice(j * PART, (j + 1) * PART)
        total[0, piece] = jnp.zeros((PART, HEAD), F32)
        for t in range(1, quads):
            @pl.when(quad - t >= 0)
            def _(t=t, j=j, piece=piece):
                later_copy(t, j).wait_recv()
                total[0, piece] = total[0, piece] + quad_recv[t - 1, piece].astype(F32)
        running = total[0, piece]
        for m in range(members):
            prefix_send[m, piece] = running.astype(BF16)
            if m < members - 1:
                value = own_total[place, piece].astype(F32)
                for t in range(1, members):
                    value = jnp.where(
                        (place - t + members) % members == m,
                        quad_parts[t - 1, piece].astype(F32), value,
                    )
                running = running + value
        for t in range(1, members):
            spread_copy(t, j).start()
        prefix_recv[place, piece] = prefix_send[place, piece]

    for j in range(PARTS):
        for t in range(1, members):
            spread_arrival(t, j).wait_recv()
    for h in range(HEADS):
        total[h] = prefix_recv[h].astype(F32)

    def project(b, carry):
        normed = []
        for c in range(BLK // ROW):
            chunk = pl.ds(pl.multiple_of(b * BLK + c * ROW, ROW), ROW)
            pieces = []
            for p in range(HEADS // 2):
                columns = slice(p * PAIR, (p + 1) * PAIR)
                state = [
                    (within[2 * b + c, 2 * p + i].astype(F32) + total[2 * p + i]).astype(BF16)
                    for i in range(2)
                ]
                attended = att[chunk, columns] + dot(qs[chunk, columns], diagonal(*state))
                for i in range(2):
                    one = attended[:, i * HEAD:(i + 1) * HEAD]
                    square = jnp.mean(one * one, axis=-1, keepdims=True)
                    pieces.append((one * lax.rsqrt(square + epsilon)).astype(BF16))
            normed.append(jnp.concatenate(pieces, axis=1))
        span = pl.ds(pl.multiple_of(b * BLK, BLK), BLK)
        mine = direct[span, :] + dot(jnp.concatenate(normed, axis=0), mixed[...])
        for c in range(BLK // ROW):
            feats[2 * b + c] = mine[c * ROW:(c + 1) * ROW].astype(BF16)
        return carry

    lax.fori_loop(0, blocks, project, 0, unroll=4)

    cell_ids = lax.broadcasted_iota(jnp.int32, (CELLS, ROW), 0)

    def across(r):
        target = wide
        for s in range(bits):
            target = target + (r // 2**s) % 2 * 2**s * (1 - 2 * ((wide // 2**s) % 2))
        return target

    def partial_pool(brick):
        marks, sources = [], []
        for m in range(most):
            row = slots[brick * most + m]
            at = jnp.maximum(row, 0)
            cells = cell_ref[pl.ds(at, 1), :] + jnp.where(row < 0, -CELLS, 0)
            marks.append(jnp.where(cell_ids == cells, 1.0, 0.0).astype(BF16))
            sources.append(feats[at])
        return dot(jnp.concatenate(marks, axis=1), jnp.concatenate(sources, axis=0))

    def turned(label, k):
        return swap_bits(label) if k == SWAPPED else label

    def piece_copy(label, bit, k):
        span = pl.ds(k * PIECE, PIECE)
        return remote(
            part_send.at[label - 1, span], part_recv.at[label - 1, span],
            sa.at[label - 1, k], ra.at[label - 1, k], across(turned(bit, k)), narrow,
        )

    odd = range(wide_count - 1, 0, -2)
    even = range(wide_count - 2, -1, -2)
    for distance in [*odd, *even]:
        pool = partial_pool(across(distance))
        for k in PIECE_ORDER:
            label = turned(distance, k)
            span = slice(k * PIECE, (k + 1) * PIECE)
            if label % 2:
                part_send[label - 1, span] = pool[span].astype(BF16)
                piece_copy(label, 1, k).start()
            else:
                own_part[label // 2, span] = pool[span]

    def halo_copy(k, dy, dx):
        if dy == 0:
            source = pooled.at[:, pl.ds(BY - EDGE if dx > 0 else 0, EDGE)]
            target = cols_recv.at[0 if dx > 0 else 1]
        else:
            span = pl.ds(BX - HALO if dy > 0 else 0, HALO)
            if dx == 0:
                source = pooled.at[span]
                target = rows_recv.at[0 if dy > 0 else 1]
            else:
                source = pooled.at[span, pl.ds(BY - EDGE if dx > 0 else 0, EDGE)]
                target = corner_recv.at[(0 if dy > 0 else 2) + (0 if dx > 0 else 1)]
        return remote(
            source, target, sh.at[k], rh.at[k],
            (wide + dy + wide_count) % wide_count, (narrow + dx + narrow_count) % narrow_count,
        )

    steps = [(dy, dx) for dy in (-1, 1) for dx in (0, -1, 1)] + [(0, -1), (0, 1)]

    def inside(dy, dx):
        return (
            (wide + dy >= 0) & (wide + dy < wide_count)
            & (narrow + dx >= 0) & (narrow + dx < narrow_count)
        )

    def send_halo(wanted):
        for k, (dy, dx) in enumerate(steps):
            if dy != wanted:
                continue

            @pl.when(inside(dy, dx))
            def _(k=k, dy=dy, dx=dx):
                halo_copy(k, dy, dx).start()

    for label in even:
        low = label & -label if label else wide_count
        for k in PIECE_ORDER:
            span = slice(k * PIECE, (k + 1) * PIECE)
            summed = own_part[label // 2, span]
            bit = 1
            while bit < low:
                piece_copy(label + bit, bit, k).wait_recv()
                summed = summed + part_recv[label + bit - 1, span].astype(F32)
                bit *= 2
            if label:
                part_send[label - 1, span] = summed.astype(BF16)
                piece_copy(label, low, k).start()
            else:
                lines = slice(k * PIECE // BY, (k + 1) * PIECE // BY)
                done = summed.astype(BF16).reshape(PIECE // BY, BY, PF)
                pooled[lines] = done
                ext[HALO + lines.start:HALO + lines.stop, EDGE:EDGE + BY, :] = done
                if k == 0:
                    send_halo(-1)
                if k == PIECES - 1:
                    send_halo(1)
    send_halo(0)

    def take_halo(across_rows):
        for k, (dy, dx) in enumerate(steps):
            if (dy != 0) != across_rows:
                continue

            @pl.when(inside(-dy, -dx))
            def _(k=k, dy=dy, dx=dx):
                halo_copy(k, dy, dx).wait_recv()
                span = slice(HALO, HALO + BX)
                if dy > 0:
                    span = slice(0, HALO)
                elif dy < 0:
                    span = slice(HALO + BX, 2 * HALO + BX)
                if dx == 0:
                    ext[span, EDGE:EDGE + BY, :] = rows_recv[0 if dy > 0 else 1]
                else:
                    columns = slice(0, EDGE) if dx > 0 else slice(EDGE + BY, WIDTH)
                    if dy == 0:
                        ext[span, columns, :] = cols_recv[0 if dx > 0 else 1]
                    else:
                        ext[span, columns, :] = corner_recv[(0 if dy > 0 else 2) + (0 if dx > 0 else 1)]

    def convolve(field, weight, start, height):
        size = height * WIDTH
        result = None
        for dx in range(3):
            shifted = None
            for dy in range(3):
                window = field[start + dy:start + dy + height].reshape(size, PF)
                term = dot(window, weight[dy, dx])
                shifted = term if shifted is None else shifted + term
            if dx != 1:
                shifted = pltpu.roll(shifted, 1 if dx == 0 else size - 1, 0)
            result = shifted if result is None else result + shifted
        return result.reshape(height, WIDTH, PF)

    def first_layer(start, height):
        active = jax.nn.gelu(convolve(ext, first, start, height), approximate=True)
        extent = (height, WIDTH, PF)
        grid_row = lax.broadcasted_iota(jnp.int32, extent, 0) + wide * BX + start - 1
        grid_column = lax.broadcasted_iota(jnp.int32, extent, 1) + narrow * BY - EDGE
        real = (
            (grid_row >= 0) & (grid_row < wide_count * BX)
            & (grid_column >= 0) & (grid_column < narrow_count * BY)
        )
        inner[start:start + height] = jnp.where(real, active, 0.0).astype(BF16)

    def second_layer(start, height):
        out_ref[start:start + height] = convolve(inner, second, start, height)[:, EDGE:EDGE + BY, :]

    loads[3].wait()
    loads[4].wait()
    take_halo(False)
    first_layer(HALO, BX - HALO)
    second_layer(HALO, BX - 2 * HALO)
    take_halo(True)
    first_layer(0, HALO)
    first_layer(BX, HALO)
    second_layer(0, HALO)
    second_layer(BX - HALO, HALO)

    for j in range(PARTS):
        for t in range(1, members):
            gather_copy(t, j).wait_send()
            spread_copy(t, j).wait_send()
        for t in range(1, quads):
            @pl.when(quad + t < quads)
            def _(t=t, j=j):
                later_copy(t, j).wait_send()

    for label in range(1, wide_count):
        for k in range(PIECES):
            piece_copy(label, label & -label, k).wait_send()
    for k, (dy, dx) in enumerate(steps):
        @pl.when(inside(dy, dx))
        def _(k=k, dy=dy, dx=dx):
            halo_copy(k, dy, dx).wait_send()


def per_device(voxels, w_qkv, w_out, w_feature, conv_first, conv_second, row_brick, cell_place):
    token_count = voxels.shape[0]
    rows = token_count // ROW
    wide_count = lax.axis_size("wide")
    narrow_count = lax.axis_size("narrow")
    blocks = token_count // BLK
    quads = wide_count // 2
    members = 2 * narrow_count
    others = max(1, quads - 1)
    most = 2 * (-(-rows // wide_count))
    anywhere = pl.BlockSpec(memory_space=pl.ANY)
    vmem = pl.BlockSpec(memory_space=pltpu.VMEM)
    smem = pl.BlockSpec(memory_space=pltpu.SMEM)
    dma = pltpu.SemaphoreType.DMA
    state = (HEAD, HEAD)
    grid = (CELLS, PF)
    scratch = [
        pltpu.VMEM(voxels.shape, BF16),
        pltpu.VMEM(w_qkv.shape, BF16),
        pltpu.VMEM(w_out.shape, BF16),
        pltpu.VMEM(w_feature.shape, BF16),
        pltpu.VMEM(conv_first.shape, BF16),
        pltpu.VMEM(conv_second.shape, BF16),
        pltpu.VMEM((token_count, 2 * D), BF16),
        pltpu.VMEM((token_count, D), BF16),
        pltpu.VMEM((token_count, D), F32),
        pltpu.VMEM((token_count, PF), F32),
        pltpu.VMEM((D, PF), BF16),
        pltpu.VMEM((rows, HEADS) + state, BF16),
        pltpu.VMEM((HEADS,) + state, F32),
        pltpu.VMEM((rows, ROW, PF), BF16),
        pltpu.SMEM((wide_count * most,), jnp.int32),
        pltpu.VMEM((members,) + state, BF16),
        pltpu.VMEM((members,) + state, BF16),
        pltpu.VMEM(state, BF16),
        pltpu.VMEM((others,) + state, BF16),
        pltpu.VMEM((members,) + state, BF16),
        pltpu.VMEM((members,) + state, BF16),
        pltpu.VMEM((wide_count - 1,) + grid, BF16),
        pltpu.VMEM((wide_count - 1,) + grid, BF16),
        pltpu.VMEM((quads,) + grid, F32),
        pltpu.VMEM((BX, BY, PF), BF16),
        pltpu.VMEM((BX + 2 * HALO, WIDTH, PF), BF16),
        pltpu.VMEM((2, HALO, BY, PF), BF16),
        pltpu.VMEM((2, BX, EDGE, PF), BF16),
        pltpu.VMEM((4, HALO, EDGE, PF), BF16),
        pltpu.VMEM((BX + 2, WIDTH, PF), BF16),
        dma((blocks,)),
        dma((6,)),
        dma((members - 1, PARTS)), dma((members - 1, PARTS)),
        dma((others, PARTS)), dma((others, PARTS)),
        dma((members - 1, PARTS)), dma((members - 1, PARTS)),
        dma((wide_count - 1, PIECES)), dma((wide_count - 1, PIECES)),
        dma((8,)), dma((8,)),
    ]
    return pl.pallas_call(
        functools.partial(kernel, wide_count, narrow_count, token_count, most),
        out_shape=jax.ShapeDtypeStruct((BX, BY, PF), F32),
        in_specs=[anywhere] * 6 + [smem, vmem],
        out_specs=vmem,
        scratch_shapes=scratch,
        compiler_params=pltpu.CompilerParams(
            collective_id=0, has_side_effects=True, vmem_limit_bytes=56 * 1024 * 1024
        ),
        name="scene_flow",
    )(
        voxels, w_qkv, w_out, w_feature, conv_first, conv_second,
        row_brick.reshape(1, rows), cell_place.reshape(rows, ROW),
    )


def solution(mesh):
    placed = (
        P(("group", "wide", "narrow"), None),
        P(),
        P(),
        P(),
        P(),
        P(),
        P(("group", "wide", "narrow"), None),
        P(("group", "wide", "narrow")),
    )
    return jax.shard_map(
        per_device,
        mesh=mesh,
        in_specs=placed,
        out_specs=P(("group", "wide"), "narrow", None),
        check_vma=False,
    )
```

time: 47.5 us -> 46 us (0.968)
  Pallas kernels: 45.2 us -> 44.1 us
    pallas_call x1, Pallas kernels: 45.2 us -> 44.1 us  [per_device(): pl.pallas_call(functools.partial(kernel, wide_count, narrow_count, token_...]
where the time goes in v1:
time: 46 us; the launch traced here: 45.8 us
  Pallas kernels  44.1 us (96%)
  local copies, waits for them, and re-layouts  1.67 us (4%)
    pallas_call x1, Pallas kernels, per_device(): pl.pallas_call(functools.partial(kernel, wide_count, narrow_count, token_...  44.1 us
    unnamed x1, local copies, waits for them, and re-layouts  1.67 us

profile of v1, /device:TPU:1, one launch (start us, length us, event | category | flops | bytes accessed | tf_op | source)
XLA Modules:
  0.0 45.8 jit_solution(10299112231043007561)
XLA Ops:
  0.0 44.1 %scene_flow.1 = f32[8,32,256]{2,1,0:T(8,128)} custom-call(bf16[2048,512]{1,0:T(8,128)(2,1)} %vox_hbm.1, bf16[512,1536]{1,0:T(8,128)(2,1)} %wqkv_hbm.1, bf16[512,512]{1,0:T(8,128)(2,1)} %wout_hbm.1, bf16[512,256]{1,0:T(8,128)(2,1)} %wfeat_hbm.1, bf16[3,3,256,256]{3,2,1,0:T(8,128)(2,1)} %first_hbm.1, bf16[3,3,256,256]{3,2,1,0:T(8,128)(2,1)} %second_hbm.1, ...), custom_call_target="tpu_custom_call" | custom-call | tf_op jit(solution)/shard_map/scene_flow/pallas_call | solution.py:539
  44.1 1.7 %copy.10 = f32[8,32,256]{2,1,0:T(8,128)} copy(f32[8,32,256]{2,1,0:T(8,128)} %scene_flow.1) | data formatting | bytes 524288

commit v2 on v1

--- a/solution.py
+++ b/solution.py
@@ -14,17 +14,18 @@
 PF = 256
 ROW = 128
 BLK = 256
+PER = BLK // ROW
 BX = 8
 BY = 32
 CELLS = BX * BY
 PAIR = 2 * HEAD
 EDGE = 16
+MIDDLE = D // 2
 WIDTH = BY + 2 * EDGE
 HALO = 2
 PIECES = 4
 PIECE = CELLS // PIECES
 PIECE_ORDER = (0, 3, 1, 2)
-SWAPPED = 2
 PARTS = 2
 PART = HEAD // PARTS
 
@@ -58,16 +59,12 @@
     )
 
 
-def swap_bits(label):
-    return label - label % 4 + 2 * (label % 2) + (label // 2) % 2
-
-
 def kernel(
     wide_count, narrow_count, token_count, most,
     vox_hbm, wqkv_hbm, wout_hbm, wfeat_hbm, first_hbm, second_hbm, brick_ref, cell_ref,
     out_ref,
     vox, wqkv, wout, wfeat, first, second,
-    kv, qs, att, direct, mixed, within, total, feats, slots,
+    kv, qs, att, direct, mixed, within, total, feats, slots, gram_upper, gram_lower, seen, base,
     own_total, quad_parts, quad_send, quad_recv, prefix_send, prefix_recv,
     part_send, part_recv, own_part,
     pooled, ext, rows_recv, cols_recv, corner_recv, inner,
@@ -100,26 +97,23 @@
         load(second_hbm, second, 4),
         load(wqkv_hbm.at[:, pl.ds(0, D)], wqkv.at[:, pl.ds(0, D)], 5),
     ]
-    loads[0].start()
     for b in range(blocks):
         load_vox(b).start()
-    for k in (5, 2, 1, 3, 4):
+    for k in (0, 5, 2, 1, 3, 4):
         loads[k].start()
 
-    everyone = wide_count * narrow_count
-    me = wide * narrow_count + narrow
     barrier = pltpu.get_barrier_semaphore()
-
-    def greet(k, carry):
-        other = (me + k) % everyone
+    beside = (wide + wide_count + 2 * side - 1) % wide_count
+    partners = [
+        (quad * 2 + (place + t) % members // narrow_count, (place + t) % narrow_count)
+        for t in range(1, members)
+    ]
+    partners += [((quad + t) % quads * 2 + side, narrow) for t in range(1, quads)]
+    partners += [(beside, n) for n in range(narrow_count)]
+    for to_wide, to_narrow in partners:
         pl.semaphore_signal(
-            barrier, inc=1,
-            device_id={"wide": other // narrow_count, "narrow": other % narrow_count},
-            device_id_type=MESH,
-        )
-        return carry
-
-    lax.fori_loop(1, everyone, greet, 0)
+            barrier, inc=1, device_id={"wide": to_wide, "narrow": to_narrow}, device_id_type=MESH
+        )
 
     def remote(source, target, send_sem, recv_sem, to_wide, to_narrow):
         return pltpu.make_async_remote_copy(
@@ -132,71 +126,104 @@
     )
     total[...] = jnp.zeros_like(total)
     ext[...] = jnp.zeros_like(ext)
+
+    def gram(start, stop):
+        span = slice(start, stop)
+        upper = dot_t(vox[span, :MIDDLE], vox[span, :])
+        lower = dot_t(vox[span, MIDDLE:], vox[span, MIDDLE:])
+        return upper, lower
+
+    half = token_count // 2
+    for b in range(blocks // 2):
+        load_vox(b).wait()
+    gram_upper[...], gram_lower[...] = gram(0, half)
+    for b in range(blocks // 2, blocks):
+        load_vox(b).wait()
+    upper, lower = gram(half, token_count)
+    upper = (gram_upper[...] + upper).astype(BF16)
+    lower = (gram_lower[...] + lower).astype(BF16)
     loads[0].wait()
-
-    def keys_values(b, carry):
-        load_vox(b).wait()
-        span = pl.ds(pl.multiple_of(b * BLK, BLK), BLK)
-        both = dot(vox[span, :], wqkv[:, D:]).astype(BF16)
-        kv[span, :] = both
+    seen[:MIDDLE] = dot(upper, wqkv[:, 2 * D:]).astype(BF16)
+    seen[MIDDLE:] = (
+        dot_t(upper[:, MIDDLE:], wqkv[:MIDDLE, 2 * D:]) + dot(lower, wqkv[MIDDLE:, 2 * D:])
+    ).astype(BF16)
+    for p in range(HEADS // 2):
+        columns = slice(p * PAIR, (p + 1) * PAIR)
+        state = dot_t(wqkv[:, D + p * PAIR:D + (p + 1) * PAIR], seen[:, columns])
+        for i in range(2):
+            corner = slice(i * HEAD, (i + 1) * HEAD)
+            own_total[2 * p + i] = state[corner, corner].astype(BF16)
+    pl.semaphore_wait(barrier, len(partners))
+
+    def part_rows(j):
+        return pl.ds(j * PART, PART)
+
+    def member(t):
+        other = (place + t) % members
+        return other, quad * 2 + other // narrow_count, other % narrow_count
+
+    def gather_copy(t, j):
+        other, to_wide, to_narrow = member(t)
+        return remote(
+            own_total.at[other, part_rows(j)], quad_parts.at[t - 1, part_rows(j)],
+            s1.at[t - 1, j], r1.at[t - 1, j], to_wide, to_narrow,
+        )
+
+    for j in range(PARTS):
+        for t in range(1, members):
+            gather_copy(t, j).start()
+
+    def inputs(b):
+        span = slice(b * BLK, (b + 1) * BLK)
+        if b == 0:
+            loads[5].wait()
+            loads[2].wait()
+        kv[span, :] = dot(vox[span, :], wqkv[:, D:]).astype(BF16)
+        query = dot(vox[span, :], wqkv[:, :D]).astype(BF16)
+        qs[PER * b:PER * (b + 1)] = query.reshape(PER, ROW, D)
+        direct[PER * b:PER * (b + 1)] = dot(vox[span, :], wfeat[...]).reshape(PER, ROW, PF)
+
+    def local(b):
         for h in range(HEADS):
-            key = both[:, h * HEAD:(h + 1) * HEAD]
-            value = both[:, D + h * HEAD:D + (h + 1) * HEAD]
-            state = dot_t(key, diagonal(value[:ROW], value[ROW:]))
+            mine = slice(h * HEAD, (h + 1) * HEAD)
+            other = slice(D + h * HEAD, D + (h + 1) * HEAD)
+            first_chunk = slice(b * BLK, b * BLK + ROW)
+            second_chunk = slice(b * BLK + ROW, (b + 1) * BLK)
+            state = dot_t(
+                kv[b * BLK:(b + 1) * BLK, mine], diagonal(kv[first_chunk, other], kv[second_chunk, other])
+            )
             before = total[h]
             within[2 * b, h] = before.astype(BF16)
             middle = before + state[:, :HEAD]
             within[2 * b + 1, h] = middle.astype(BF16)
             total[h] = middle + state[:, HEAD:]
-        return carry
-
-    lax.fori_loop(0, blocks, keys_values, 0, unroll=4)
-
-    for h in range(HEADS):
-        own_total[h] = total[h].astype(BF16)
-    pl.semaphore_wait(barrier, everyone - 1)
-
-    def part_rows(j):
-        return pl.ds(j * PART, PART)
-
-    def member(t):
-        other = (place + t) % members
-        return other, quad * 2 + other // narrow_count, other % narrow_count
-
-    def gather_copy(t, j):
-        other, to_wide, to_narrow = member(t)
-        return remote(
-            own_total.at[other, part_rows(j)], quad_parts.at[t - 1, part_rows(j)],
-            s1.at[t - 1, j], r1.at[t - 1, j], to_wide, to_narrow,
-        )
-
-    for j in range(PARTS):
-        for t in range(1, members):
-            gather_copy(t, j).start()
-
-    def local(b, carry):
-        span = pl.ds(pl.multiple_of(b * BLK, BLK), BLK)
-        query = dot(vox[span, :], wqkv[:, :D]).astype(BF16)
-        qs[span, :] = query
-        direct[span, :] = dot(vox[span, :], wfeat[...])
-        for c in range(BLK // ROW):
-            chunk = pl.ds(pl.multiple_of(b * BLK + c * ROW, ROW), ROW)
+        scores = {}
+        for c in range(PER):
+            row = b * PER + c
+            chunk = slice(row * ROW, (row + 1) * ROW)
             for p in range(HEADS // 2):
-                columns = slice(p * PAIR, (p + 1) * PAIR)
                 low, high = 2 * p * HEAD, (2 * p + 1) * HEAD
                 keys = diagonal(kv[chunk, low:low + HEAD], kv[chunk, high:high + HEAD])
-                scores = dot_nt(query[c * ROW:(c + 1) * ROW, columns], keys)
-                scores = jnp.where(causal, scores, 0.0).astype(BF16)
-                values = diagonal(
-                    kv[chunk, D + low:D + low + HEAD], kv[chunk, D + high:D + high + HEAD]
-                )
-                att[chunk, columns] = dot(scores, values)
-        return carry
-
-    cut = blocks // 2
-    loads[5].wait()
-    loads[2].wait()
-    lax.fori_loop(0, cut, local, 0, unroll=2)
+                both = dot_nt(qs[row, :, p * PAIR:(p + 1) * PAIR], keys)
+                scores[c, p] = jnp.where(causal, both, 0.0).astype(BF16)
+        for c in range(PER):
+            row = b * PER + c
+            chunk = slice(row * ROW, (row + 1) * ROW)
+            for p in range(HEADS // 2):
+                low, high = D + 2 * p * HEAD, D + (2 * p + 1) * HEAD
+                values = diagonal(kv[chunk, low:low + HEAD], kv[chunk, high:high + HEAD])
+                att[row, :, p * PAIR:(p + 1) * PAIR] = dot(scores[c, p], values)
+
+    def within_device(start, stop):
+        for b in range(start, stop):
+            if b < blocks:
+                inputs(b)
+            if b > 0:
+                local(b - 1)
+
+    cut_one = blocks // 2
+    cut_two = blocks
+    within_device(0, cut_one)
 
     def later_copy(t, j):
         return remote(
@@ -218,7 +245,7 @@
             def _(t=t, j=j):
                 later_copy(t, j).start()
 
-    lax.fori_loop(cut, blocks, local, 0, unroll=2)
+    within_device(cut_one, cut_two)
     loads[1].wait()
     mixed[...] = dot(wout[...], wfeat[...]).astype(BF16)
 
@@ -251,13 +278,13 @@
 
     for j in range(PARTS):
         piece = slice(j * PART, (j + 1) * PART)
-        total[0, piece] = jnp.zeros((PART, HEAD), F32)
+        base[piece] = jnp.zeros((PART, HEAD), F32)
         for t in range(1, quads):
             @pl.when(quad - t >= 0)
             def _(t=t, j=j, piece=piece):
                 later_copy(t, j).wait_recv()
-                total[0, piece] = total[0, piece] + quad_recv[t - 1, piece].astype(F32)
-        running = total[0, piece]
+                base[piece] = base[piece] + quad_recv[t - 1, piece].astype(F32)
+        running = base[piece]
         for m in range(members):
             prefix_send[m, piece] = running.astype(BF16)
             if m < members - 1:
@@ -272,36 +299,49 @@
             spread_copy(t, j).start()
         prefix_recv[place, piece] = prefix_send[place, piece]
 
+    within_device(cut_two, blocks + 1)
+
     for j in range(PARTS):
         for t in range(1, members):
             spread_arrival(t, j).wait_recv()
     for h in range(HEADS):
         total[h] = prefix_recv[h].astype(F32)
 
-    def project(b, carry):
-        normed = []
-        for c in range(BLK // ROW):
-            chunk = pl.ds(pl.multiple_of(b * BLK + c * ROW, ROW), ROW)
-            pieces = []
+    def state_of(row, p):
+        return diagonal(*[
+            (within[row, 2 * p + i].astype(F32) + total[2 * p + i]).astype(BF16) for i in range(2)
+        ])
+
+    def scaled(one):
+        square = jnp.mean(one * one, axis=-1, keepdims=True)
+        return (one * lax.rsqrt(square + epsilon)).astype(BF16)
+
+    def attend(b):
+        for row in range(PER * b, PER * (b + 1)):
             for p in range(HEADS // 2):
                 columns = slice(p * PAIR, (p + 1) * PAIR)
-                state = [
-                    (within[2 * b + c, 2 * p + i].astype(F32) + total[2 * p + i]).astype(BF16)
-                    for i in range(2)
-                ]
-                attended = att[chunk, columns] + dot(qs[chunk, columns], diagonal(*state))
-                for i in range(2):
-                    one = attended[:, i * HEAD:(i + 1) * HEAD]
-                    square = jnp.mean(one * one, axis=-1, keepdims=True)
-                    pieces.append((one * lax.rsqrt(square + epsilon)).astype(BF16))
-            normed.append(jnp.concatenate(pieces, axis=1))
-        span = pl.ds(pl.multiple_of(b * BLK, BLK), BLK)
-        mine = direct[span, :] + dot(jnp.concatenate(normed, axis=0), mixed[...])
-        for c in range(BLK // ROW):
-            feats[2 * b + c] = mine[c * ROW:(c + 1) * ROW].astype(BF16)
-        return carry
-
-    lax.fori_loop(0, blocks, project, 0, unroll=4)
+                att[row, :, columns] += dot(qs[row, :, columns], state_of(row, p))
+
+    def normalise(b):
+        for row in range(PER * b, PER * (b + 1)):
+            for h in range(HEADS):
+                mine = slice(h * HEAD, (h + 1) * HEAD)
+                qs[row, :, mine] = scaled(att[row, :, mine])
+
+    def finish(b):
+        span = slice(PER * b, PER * (b + 1))
+        normed = qs[span].reshape(BLK, D)
+        mine = direct[span].reshape(BLK, PF) + dot(normed, mixed[...])
+        feats[span] = mine.astype(BF16).reshape(PER, ROW, PF)
+
+    def project():
+        for b in range(blocks + 2):
+            if b < blocks:
+                attend(b)
+            if 0 < b <= blocks:
+                normalise(b - 1)
+            if b > 1:
+                finish(b - 2)
 
     cell_ids = lax.broadcasted_iota(jnp.int32, (CELLS, ROW), 0)
 
@@ -311,38 +351,52 @@
             target = target + (r // 2**s) % 2 * 2**s * (1 - 2 * ((wide // 2**s) % 2))
         return target
 
-    def partial_pool(brick):
-        marks, sources = [], []
+    def named_rows(brick):
+        marks, chosen = [], []
         for m in range(most):
-            row = slots[brick * most + m]
-            at = jnp.maximum(row, 0)
-            cells = cell_ref[pl.ds(at, 1), :] + jnp.where(row < 0, -CELLS, 0)
+            named = slots[brick * most + m]
+            row = jnp.maximum(named, 0)
+            cells = cell_ref[pl.ds(row, 1), :] + jnp.where(named < 0, -CELLS, 0)
             marks.append(jnp.where(cell_ids == cells, 1.0, 0.0).astype(BF16))
-            sources.append(feats[at])
-        return dot(jnp.concatenate(marks, axis=1), jnp.concatenate(sources, axis=0))
-
-    def turned(label, k):
-        return swap_bits(label) if k == SWAPPED else label
+            chosen.append(row)
+        return jnp.concatenate(marks, axis=1), chosen
+
+    def pool_ready(brick):
+        marks, chosen = named_rows(brick)
+        return dot(marks, jnp.concatenate([feats[row] for row in chosen], axis=0))
+
+    def pool_afresh(brick):
+        marks, chosen = named_rows(brick)
+        normed, plain = [], []
+        for row in chosen:
+            pieces = []
+            for p in range(HEADS // 2):
+                columns = slice(p * PAIR, (p + 1) * PAIR)
+                attended = att[row, :, columns] + dot(qs[row, :, columns], state_of(row, p))
+                pieces += [scaled(attended[:, i * HEAD:(i + 1) * HEAD]) for i in range(2)]
+            normed.append(jnp.concatenate(pieces, axis=1))
+            plain.append(direct[row])
+        features = jnp.concatenate(plain, axis=0) + dot(jnp.concatenate(normed, axis=0), mixed[...])
+        return dot(marks, features.astype(BF16))
 
     def piece_copy(label, bit, k):
         span = pl.ds(k * PIECE, PIECE)
         return remote(
             part_send.at[label - 1, span], part_recv.at[label - 1, span],
-            sa.at[label - 1, k], ra.at[label - 1, k], across(turned(bit, k)), narrow,
-        )
-
-    odd = range(wide_count - 1, 0, -2)
-    even = range(wide_count - 2, -1, -2)
-    for distance in [*odd, *even]:
-        pool = partial_pool(across(distance))
+            sa.at[label - 1, k], ra.at[label - 1, k], across(bit), narrow,
+        )
+
+    def send_partner(label, pool):
+        part_send[label - 1] = pool.astype(BF16)
         for k in PIECE_ORDER:
-            label = turned(distance, k)
-            span = slice(k * PIECE, (k + 1) * PIECE)
-            if label % 2:
-                part_send[label - 1, span] = pool[span].astype(BF16)
-                piece_copy(label, 1, k).start()
-            else:
-                own_part[label // 2, span] = pool[span]
+            piece_copy(label, 1, k).start()
+
+    send_partner(wide_count - 1, pool_afresh(across(wide_count - 1)))
+    project()
+    for label in range(wide_count - 3, 0, -2):
+        send_partner(label, pool_ready(across(label)))
+    for label in range(wide_count - 2, -1, -2):
+        own_part[label // 2] = pool_ready(across(label))
 
     def halo_copy(k, dy, dx):
         if dy == 0:
@@ -378,7 +432,7 @@
             def _(k=k, dy=dy, dx=dx):
                 halo_copy(k, dy, dx).start()
 
-    for label in even:
+    for label in range(wide_count - 2, -1, -2):
         low = label & -label if label else wide_count
         for k in PIECE_ORDER:
             span = slice(k * PIECE, (k + 1) * PIECE)
@@ -505,14 +559,18 @@
         pltpu.VMEM(conv_first.shape, BF16),
         pltpu.VMEM(conv_second.shape, BF16),
         pltpu.VMEM((token_count, 2 * D), BF16),
-        pltpu.VMEM((token_count, D), BF16),
-        pltpu.VMEM((token_count, D), F32),
-        pltpu.VMEM((token_count, PF), F32),
+        pltpu.VMEM((rows, ROW, D), BF16),
+        pltpu.VMEM((rows, ROW, D), F32),
+        pltpu.VMEM((rows, ROW, PF), F32),
         pltpu.VMEM((D, PF), BF16),
         pltpu.VMEM((rows, HEADS) + state, BF16),
         pltpu.VMEM((HEADS,) + state, F32),
         pltpu.VMEM((rows, ROW, PF), BF16),
         pltpu.SMEM((wide_count * most,), jnp.int32),
+        pltpu.VMEM((MIDDLE, D), F32),
+        pltpu.VMEM((MIDDLE, MIDDLE), F32),
+        pltpu.VMEM((D, D), BF16),
+        pltpu.VMEM(state, F32),
         pltpu.VMEM((members,) + state, BF16),
         pltpu.VMEM((members,) + state, BF16),
         pltpu.VMEM(state, BF16),

time: 46 us -> 41.2 us (0.90)
  Pallas kernels: 44.1 us -> 39.4 us
    pallas_call x1, Pallas kernels: 44.1 us -> 39.4 us  [per_device(): pl.pallas_call(functools.partial(kernel, wide_count, narrow_count, token_...]
where the time goes in v2:
time: 41.2 us; the launch traced here: 41 us
  Pallas kernels  39.4 us (96%)
  local copies, waits for them, and re-layouts  1.67 us (4%)
    pallas_call x1, Pallas kernels, per_device(): pl.pallas_call(functools.partial(kernel, wide_count, narrow_count, token_...  39.4 us
    unnamed x1, local copies, waits for them, and re-layouts  1.67 us

profile of v2, /device:TPU:1, one launch (start us, length us, event | category | flops | bytes accessed | tf_op | source)
XLA Modules:
  0.0 41.0 jit_solution(4219618912590690032)
XLA Ops:
  0.0 39.4 %scene_flow.1 = f32[8,32,256]{2,1,0:T(8,128)} custom-call(bf16[2048,512]{1,0:T(8,128)(2,1)} %vox_hbm.1, bf16[512,1536]{1,0:T(8,128)(2,1)} %wqkv_hbm.1, bf16[512,512]{1,0:T(8,128)(2,1)} %wout_hbm.1, bf16[512,256]{1,0:T(8,128)(2,1)} %wfeat_hbm.1, bf16[3,3,256,256]{3,2,1,0:T(8,128)(2,1)} %first_hbm.1, bf16[3,3,256,256]{3,2,1,0:T(8,128)(2,1)} %second_hbm.1, ...), custom_call_target="tpu_custom_call" | custom-call | tf_op jit(solution)/shard_map/scene_flow/pallas_call | solution.py:597
  39.4 1.7 %copy.10 = f32[8,32,256]{2,1,0:T(8,128)} copy(f32[8,32,256]{2,1,0:T(8,128)} %scene_flow.1) | data formatting | bytes 524288

commit v3 on v2

--- a/solution.py
+++ b/solution.py
@@ -222,7 +222,7 @@
                 local(b - 1)
 
     cut_one = blocks // 2
-    cut_two = blocks
+    cut_two = blocks - 2
     within_device(0, cut_one)
 
     def later_copy(t, j):
@@ -391,13 +391,6 @@
         for k in PIECE_ORDER:
             piece_copy(label, 1, k).start()
 
-    send_partner(wide_count - 1, pool_afresh(across(wide_count - 1)))
-    project()
-    for label in range(wide_count - 3, 0, -2):
-        send_partner(label, pool_ready(across(label)))
-    for label in range(wide_count - 2, -1, -2):
-        own_part[label // 2] = pool_ready(across(label))
-
     def halo_copy(k, dy, dx):
         if dy == 0:
             source = pooled.at[:, pl.ds(BY - EDGE if dx > 0 else 0, EDGE)]
@@ -432,7 +425,10 @@
             def _(k=k, dy=dy, dx=dx):
                 halo_copy(k, dy, dx).start()
 
-    for label in range(wide_count - 2, -1, -2):
+    def pool_own(label):
+        own_part[label // 2] = pool_ready(across(label))
+
+    def reduce(label):
         low = label & -label if label else wide_count
         for k in PIECE_ORDER:
             span = slice(k * PIECE, (k + 1) * PIECE)
@@ -454,6 +450,19 @@
                     send_halo(-1)
                 if k == PIECES - 1:
                     send_halo(1)
+
+    top = wide_count - 1
+    send_partner(top, pool_afresh(across(top)))
+    project()
+    send_partner(top - 2, pool_ready(across(top - 2)))
+    pool_own(top - 1)
+    reduce(top - 1)
+    for label in range(top - 4, 0, -2):
+        send_partner(label, pool_ready(across(label)))
+    for label in range(top - 3, -1, -2):
+        pool_own(label)
+    for label in range(top - 3, -1, -2):
+        reduce(label)
     send_halo(0)
 
     def take_halo(across_rows):

time: 41.2 us -> 39.7 us (0.964)
  Pallas kernels: 39.4 us -> 37.8 us
    pallas_call x1, Pallas kernels: 39.4 us -> 37.8 us  [per_device(): pl.pallas_call(functools.partial(kernel, wide_count, narrow_count, token_...]
where the time goes in v3:
time: 39.7 us; the launch traced here: 39.5 us
  Pallas kernels  37.8 us (95%)
  local copies, waits for them, and re-layouts  1.67 us (4%)
    pallas_call x1, Pallas kernels, per_device(): pl.pallas_call(functools.partial(kernel, wide_count, narrow_count, token_...  37.8 us
    unnamed x1, local copies, waits for them, and re-layouts  1.67 us

profile of v3, /device:TPU:1, one launch (start us, length us, event | category | flops | bytes accessed | tf_op | source)
XLA Modules:
  0.0 39.5 jit_solution(10281259578240616547)
XLA Ops:
  0.0 37.8 %scene_flow.1 = f32[8,32,256]{2,1,0:T(8,128)} custom-call(bf16[2048,512]{1,0:T(8,128)(2,1)} %vox_hbm.1, bf16[512,1536]{1,0:T(8,128)(2,1)} %wqkv_hbm.1, bf16[512,512]{1,0:T(8,128)(2,1)} %wout_hbm.1, bf16[512,256]{1,0:T(8,128)(2,1)} %wfeat_hbm.1, bf16[3,3,256,256]{3,2,1,0:T(8,128)(2,1)} %first_hbm.1, bf16[3,3,256,256]{3,2,1,0:T(8,128)(2,1)} %second_hbm.1, ...), custom_call_target="tpu_custom_call" | custom-call | tf_op jit(solution)/shard_map/scene_flow/pallas_call | solution.py:606
  37.8 1.7 %copy.10 = f32[8,32,256]{2,1,0:T(8,128)} copy(f32[8,32,256]{2,1,0:T(8,128)} %scene_flow.1) | data formatting | bytes 524288

commit v4 on v3

--- a/solution.py
+++ b/solution.py
@@ -19,7 +19,7 @@
 BY = 32
 CELLS = BX * BY
 PAIR = 2 * HEAD
-EDGE = 16
+EDGE = 8
 MIDDLE = D // 2
 WIDTH = BY + 2 * EDGE
 HALO = 2

time: 39.7 us -> 39.3 us (0.990)
  Pallas kernels: 37.8 us -> 37.4 us
where the time goes in v4:
time: 39.3 us; the launch traced here: 39.1 us
  Pallas kernels  37.4 us (95%)
  local copies, waits for them, and re-layouts  1.67 us (4%)
    pallas_call x1, Pallas kernels, per_device(): pl.pallas_call(functools.partial(kernel, wide_count, narrow_count, token_...  37.4 us
    unnamed x1, local copies, waits for them, and re-layouts  1.67 us

profile of v4, /device:TPU:1, one launch (start us, length us, event | category | flops | bytes accessed | tf_op | source)
XLA Modules:
  0.0 39.1 jit_solution(13749619124528431326)
XLA Ops:
  0.0 37.4 %scene_flow.1 = f32[8,32,256]{2,1,0:T(8,128)} custom-call(bf16[2048,512]{1,0:T(8,128)(2,1)} %vox_hbm.1, bf16[512,1536]{1,0:T(8,128)(2,1)} %wqkv_hbm.1, bf16[512,512]{1,0:T(8,128)(2,1)} %wout_hbm.1, bf16[512,256]{1,0:T(8,128)(2,1)} %wfeat_hbm.1, bf16[3,3,256,256]{3,2,1,0:T(8,128)(2,1)} %first_hbm.1, bf16[3,3,256,256]{3,2,1,0:T(8,128)(2,1)} %second_hbm.1, ...), custom_call_target="tpu_custom_call" | custom-call | tf_op jit(solution)/shard_map/scene_flow/pallas_call | solution.py:606
  37.4 1.7 %copy.10 = f32[8,32,256]{2,1,0:T(8,128)} copy(f32[8,32,256]{2,1,0:T(8,128)} %scene_flow.1) | data formatting | bytes 524288

commit v5 on v4

--- a/solution.py
+++ b/solution.py
@@ -64,7 +64,7 @@
     vox_hbm, wqkv_hbm, wout_hbm, wfeat_hbm, first_hbm, second_hbm, brick_ref, cell_ref,
     out_ref,
     vox, wqkv, wout, wfeat, first, second,
-    kv, qs, att, direct, mixed, within, total, feats, slots, gram_upper, gram_lower, seen, base,
+    kv, qs, att, direct, mixed, within, total, feats, slots, gram_upper, gram_lower, seen, base, early,
     own_total, quad_parts, quad_send, quad_recv, prefix_send, prefix_recv,
     part_send, part_recv, own_part,
     pooled, ext, rows_recv, cols_recv, corner_recv, inner,
@@ -301,48 +301,6 @@
 
     within_device(cut_two, blocks + 1)
 
-    for j in range(PARTS):
-        for t in range(1, members):
-            spread_arrival(t, j).wait_recv()
-    for h in range(HEADS):
-        total[h] = prefix_recv[h].astype(F32)
-
-    def state_of(row, p):
-        return diagonal(*[
-            (within[row, 2 * p + i].astype(F32) + total[2 * p + i]).astype(BF16) for i in range(2)
-        ])
-
-    def scaled(one):
-        square = jnp.mean(one * one, axis=-1, keepdims=True)
-        return (one * lax.rsqrt(square + epsilon)).astype(BF16)
-
-    def attend(b):
-        for row in range(PER * b, PER * (b + 1)):
-            for p in range(HEADS // 2):
-                columns = slice(p * PAIR, (p + 1) * PAIR)
-                att[row, :, columns] += dot(qs[row, :, columns], state_of(row, p))
-
-    def normalise(b):
-        for row in range(PER * b, PER * (b + 1)):
-            for h in range(HEADS):
-                mine = slice(h * HEAD, (h + 1) * HEAD)
-                qs[row, :, mine] = scaled(att[row, :, mine])
-
-    def finish(b):
-        span = slice(PER * b, PER * (b + 1))
-        normed = qs[span].reshape(BLK, D)
-        mine = direct[span].reshape(BLK, PF) + dot(normed, mixed[...])
-        feats[span] = mine.astype(BF16).reshape(PER, ROW, PF)
-
-    def project():
-        for b in range(blocks + 2):
-            if b < blocks:
-                attend(b)
-            if 0 < b <= blocks:
-                normalise(b - 1)
-            if b > 1:
-                finish(b - 2)
-
     cell_ids = lax.broadcasted_iota(jnp.int32, (CELLS, ROW), 0)
 
     def across(r):
@@ -361,12 +319,56 @@
             chosen.append(row)
         return jnp.concatenate(marks, axis=1), chosen
 
+    early[...] = named_rows(across(wide_count - 1))[0]
+
+    for j in range(PARTS):
+        for t in range(1, members):
+            spread_arrival(t, j).wait_recv()
+    for h in range(HEADS):
+        total[h] = prefix_recv[h].astype(F32)
+
+    def state_of(row, p):
+        return diagonal(*[
+            (within[row, 2 * p + i].astype(F32) + total[2 * p + i]).astype(BF16) for i in range(2)
+        ])
+
+    def scaled(one):
+        square = jnp.mean(one * one, axis=-1, keepdims=True)
+        return (one * lax.rsqrt(square + epsilon)).astype(BF16)
+
+    def attend(b):
+        for row in range(PER * b, PER * (b + 1)):
+            for p in range(HEADS // 2):
+                columns = slice(p * PAIR, (p + 1) * PAIR)
+                att[row, :, columns] += dot(qs[row, :, columns], state_of(row, p))
+
+    def normalise(b):
+        for row in range(PER * b, PER * (b + 1)):
+            for h in range(HEADS):
+                mine = slice(h * HEAD, (h + 1) * HEAD)
+                qs[row, :, mine] = scaled(att[row, :, mine])
+
+    def finish(b):
+        span = slice(PER * b, PER * (b + 1))
+        normed = qs[span].reshape(BLK, D)
+        mine = direct[span].reshape(BLK, PF) + dot(normed, mixed[...])
+        feats[span] = mine.astype(BF16).reshape(PER, ROW, PF)
+
+    def project():
+        for b in range(blocks + 2):
+            if b < blocks:
+                attend(b)
+            if 0 < b <= blocks:
+                normalise(b - 1)
+            if b > 1:
+                finish(b - 2)
+
     def pool_ready(brick):
         marks, chosen = named_rows(brick)
         return dot(marks, jnp.concatenate([feats[row] for row in chosen], axis=0))
 
     def pool_afresh(brick):
-        marks, chosen = named_rows(brick)
+        chosen = named_rows(brick)[1]
         normed, plain = [], []
         for row in chosen:
             pieces = []
@@ -377,7 +379,7 @@
             normed.append(jnp.concatenate(pieces, axis=1))
             plain.append(direct[row])
         features = jnp.concatenate(plain, axis=0) + dot(jnp.concatenate(normed, axis=0), mixed[...])
-        return dot(marks, features.astype(BF16))
+        return dot(early[...], features.astype(BF16))
 
     def piece_copy(label, bit, k):
         span = pl.ds(k * PIECE, PIECE)
@@ -580,6 +582,7 @@
         pltpu.VMEM((MIDDLE, MIDDLE), F32),
         pltpu.VMEM((D, D), BF16),
         pltpu.VMEM(state, F32),
+        pltpu.VMEM((CELLS, most * ROW), BF16),
         pltpu.VMEM((members,) + state, BF16),
         pltpu.VMEM((members,) + state, BF16),
         pltpu.VMEM(state, BF16),

time: 39.3 us -> 39.3 us (level)
  no operation moved by 1% of the time
where the time goes in v5:
time: 39.3 us; the launch traced here: 39.1 us
  Pallas kernels  37.4 us (95%)
  local copies, waits for them, and re-layouts  1.67 us (4%)
    pallas_call x1, Pallas kernels, per_device(): pl.pallas_call(functools.partial(kernel, wide_count, narrow_count, token_...  37.4 us
    unnamed x1, local copies, waits for them, and re-layouts  1.67 us

profile of v5, /device:TPU:1, one launch (start us, length us, event | category | flops | bytes accessed | tf_op | source)
XLA Modules:
  0.0 39.1 jit_solution(6632782574381876354)
XLA Ops:
  0.0 37.4 %scene_flow.1 = f32[8,32,256]{2,1,0:T(8,128)} custom-call(bf16[2048,512]{1,0:T(8,128)(2,1)} %vox_hbm.1, bf16[512,1536]{1,0:T(8,128)(2,1)} %wqkv_hbm.1, bf16[512,512]{1,0:T(8,128)(2,1)} %wout_hbm.1, bf16[512,256]{1,0:T(8,128)(2,1)} %wfeat_hbm.1, bf16[3,3,256,256]{3,2,1,0:T(8,128)(2,1)} %first_hbm.1, bf16[3,3,256,256]{3,2,1,0:T(8,128)(2,1)} %second_hbm.1, ...), custom_call_target="tpu_custom_call" | custom-call | tf_op jit(solution)/shard_map/scene_flow/pallas_call | solution.py:609
  37.4 1.7 %copy.10 = f32[8,32,256]{2,1,0:T(8,128)} copy(f32[8,32,256]{2,1,0:T(8,128)} %scene_flow.1) | data formatting | bytes 524288
